TPU v7x, 256 devices: a whole 4x4x8 slice. The times are simulated.
256 devices in a mesh: seq: 32 (over y, x, core), head: 8 (over z).
Axes of the slice: x: 4, y: 4, z: 8, core: 2. Of those that a mesh axis runs over, the one named last changes fastest.
Arguments:
- queries: bfloat16 [32768, 8192], P(('seq', 'head')), may hold values from -6 to 6
- key_vectors: bfloat16 [32768, 8192], P(('seq', 'head')), may hold values from -6 to 6
- value_vectors: bfloat16 [32768, 8192], P(('seq', 'head')), may hold values from -6 to 6
- out_gain: float32 [64, 128], P('head'), may hold values from 0.1 to 1.9
Outputs:
- attended: bfloat16 [32768, 8192], P(('seq', 'head'))
All inputs are finite; a program needn't handle non-finite values.
Results may differ from a plain program's by a relative error of at most 0.0049.
Values may be sent and summed in bfloat16 or wider, within the bound.
A program may use at most 128 MiB of HBM per device.

v0:
```python
import jax
import jax.numpy as jnp
from jax import lax
from jax.sharding import PartitionSpec as P

HEADS = 64
HD = 128


def shifted(block, axis, distance):
    count = lax.axis_size(axis)
    return lax.ppermute(block, axis, [(i, i + distance) for i in range(count - distance)])


def seq_exclusive(own):
    count = lax.axis_size("seq")
    total = own
    distance = 1
    while distance < count:
        total = total + shifted(total, "seq", distance)
        distance *= 2
    return shifted(total, "seq", 1)


def per_device(queries, key_vectors, value_vectors, out_gain):
    tokens = queries.shape[0]
    query_heads = queries.reshape(tokens, HEADS, HD)
    key_heads = key_vectors.reshape(tokens, HEADS, HD)
    value_heads = value_vectors.reshape(tokens, HEADS, HD)
    states = jnp.einsum("bhd,bhe->hde", key_heads, value_heads, preferred_element_type=jnp.float32)
    gathered = lax.all_to_all(
        states.astype(jnp.bfloat16).reshape(8, HEADS // 8, HD, HD),
        "head",
        split_axis=0,
        concat_axis=0,
        tiled=True,
    ).astype(jnp.float32)
    gain = lax.all_gather(out_gain, "head", axis=0, tiled=True)
    prefix = seq_exclusive(jnp.sum(gathered, axis=0))
    running = prefix
    parts = []
    for z in range(8):
        parts.append(running.astype(jnp.bfloat16))
        running = running + gathered[z]
    carried = lax.all_to_all(jnp.stack(parts), "head", split_axis=0, concat_axis=0, tiled=True)
    carried = carried.reshape(HEADS, HD, HD)
    inter = jnp.einsum("bhd,hde->bhe", query_heads, carried, preferred_element_type=jnp.float32)
    scores = jnp.einsum("bhd,chd->hbc", query_heads, key_heads, preferred_element_type=jnp.float32)
    causal = jnp.arange(tokens)[:, None] >= jnp.arange(tokens)[None, :]
    scores = jnp.where(causal[None], scores, jnp.float32(0.0)).astype(jnp.bfloat16)
    intra = jnp.einsum("hbc,chd->bhd", scores, value_heads, preferred_element_type=jnp.float32)
    raw = inter + intra
    scale = lax.rsqrt(jnp.mean(raw * raw, axis=-1, keepdims=True) + 1e-06)
    normed = (raw * scale * gain[None]).astype(jnp.bfloat16)
    return normed.reshape(tokens, HEADS * HD)


def solution(mesh):
    return jax.shard_map(
        per_device,
        mesh=mesh,
        in_specs=(
            P(("seq", "head"), None),
            P(("seq", "head"), None),
            P(("seq", "head"), None),
            P("head", None),
        ),
        out_specs=P(("seq", "head"), None),
        check_vma=False,
    )
```

profile of v0, /device:TPU:56, one launch (start us, length us, event | category | flops | bytes accessed | tf_op | source)
XLA Modules:
  0.0 247.2 jit_solution(813136822619654408)
XLA Ops:
  0.0 4.2 %copy.11 = bf16[128,8192]{0,1:T(8,128)(2,1)} copy(bf16[128,8192]{1,0:T(8,128)(2,1)} %param.5) | data formatting | bytes 4194304 | tf_op jit(solution)/shard_map/reshape | solution.py:28
  4.2 4.1 %copy.12 = bf16[128,8192]{0,1:T(8,128)(2,1)} copy(bf16[128,8192]{1,0:T(8,128)(2,1)} %param.6) | data formatting | bytes 4194304 | tf_op jit(solution)/shard_map/reshape | solution.py:29
  8.3 3.8 %convolution_convert_fusion = bf16[64,128,128]{2,1,0:T(8,128)(2,1)S(1)} fusion(bf16[128,64,128]{0,2,1:T(8,128)(2,1)} %bitcast.108, bf16[128,64,128]{0,2,1:T(8,128)(2,1)} %bitcast.110), kind=kOutput, calls=%fused_computation.7 | convolution fusion | flops 269484032 | bytes 6291456 | tf_op jit(solution)/shard_map/bhd,bhe->hde/dot_general | solution.py:30
  12.1 58.1 %all_to_all.10 = bf16[8,8,128,128]{3,2,1,0:T(8,128)(2,1)S(1)} all-to-all(bf16[8,8,128,128]{3,2,1,0:T(8,128)(2,1)S(1)} %bitcast.113), channel_id=1, replica_groups=mesh['seq'=32,'head'=8] {'head'}, dimensions={0} | all-to-all | bytes 4194304 | tf_op jit(solution)/shard_map/all_to_all | solution.py:31
  70.5 1.9 collective-permute-start
  72.5 10.7 %collective-permute-done = f32[8,128,128]{2,1,0:T(8,128)S(1)} collective-permute-done((f32[8,128,128]{2,1,0:T(8,128)S(1)}, f32[8,128,128]{2,1,0:T(8,128)S(1)}, u32[]{:S(2)}, u32[]{:S(2)}) %collective-permute-start) | collective-permute-done | bytes 524320 | tf_op jit(solution)/shard_map/ppermute | solution.py:12
  83.2 1.9 collective-permute-start.1
  85.1 12.9 %collective-permute-done.1 = f32[8,128,128]{2,1,0:T(8,128)S(1)} collective-permute-done((f32[8,128,128]{2,1,0:T(8,128)S(1)}, f32[8,128,128]{2,1,0:T(8,128)S(1)}, u32[]{:S(2)}, u32[]{:S(2)}) %collective-permute-start.1) | collective-permute-done | bytes 524320 | tf_op jit(solution)/shard_map/ppermute | solution.py:12
  98.1 2.5 %collective-permute-start.2 = (f32[8,128,128]{2,1,0:T(8,128)S(1)}, f32[8,128,128]{2,1,0:T(8,128)S(1)}, u32[]{:S(2)}, u32[]{:S(2)}) collective-permute-start(f32[8,128,128]{2,1,0:T(8,128)S(1)} %add.51), channel_id=1, source_target_pairs={{0,32},{8,40},{16,48},{24,56},{32,64},{40,72},{48,80},{56,88},{64,... | collective-permute-start | bytes 1572872 | tf_op jit(solution)/shard_map/ppermute | solution.py:12
  100.7 11.8 %collective-permute-done.2 = f32[8,128,128]{2,1,0:T(8,128)S(1)} collective-permute-done((f32[8,128,128]{2,1,0:T(8,128)S(1)}, f32[8,128,128]{2,1,0:T(8,128)S(1)}, u32[]{:S(2)}, u32[]{:S(2)}) %collective-permute-start.2) | collective-permute-done | bytes 524320 | tf_op jit(solution)/shard_map/ppermute | solution.py:12
  112.5 1.3 collective-permute-start.3
  113.8 9.9 %collective-permute-done.3 = f32[8,128,128]{2,1,0:T(8,128)S(1)} collective-permute-done((f32[8,128,128]{2,1,0:T(8,128)S(1)}, f32[8,128,128]{2,1,0:T(8,128)S(1)}, u32[]{:S(2)}, u32[]{:S(2)}) %collective-permute-start.3) | collective-permute-done | bytes 524320 | tf_op jit(solution)/shard_map/ppermute | solution.py:12
  123.7 1.3 collective-permute-start.4
  125.0 11.3 %collective-permute-done.4 = f32[8,128,128]{2,1,0:T(8,128)S(1)} collective-permute-done((f32[8,128,128]{2,1,0:T(8,128)S(1)}, f32[8,128,128]{2,1,0:T(8,128)S(1)}, u32[]{:S(2)}, u32[]{:S(2)}) %collective-permute-start.4) | collective-permute-done | bytes 524320 | tf_op jit(solution)/shard_map/ppermute | solution.py:12
  136.3 1.9 collective-permute-start.5
  138.8 10.2 %collective-permute-done.5 = f32[8,128,128]{2,1,0:T(8,128)S(1)} collective-permute-done((f32[8,128,128]{2,1,0:T(8,128)S(1)}, f32[8,128,128]{2,1,0:T(8,128)S(1)}, u32[]{:S(2)}, u32[]{:S(2)}) %collective-permute-start.5) | collective-permute-done | bytes 524320 | tf_op jit(solution)/shard_map/ppermute | solution.py:12
  152.0 0.8 bitcast_dynamic-update-slice_fusion.2
  154.4 0.8 fusion.16
  155.2 5.8 %all-to-all-start.1 = ((bf16[8,8,128,128]{3,2,1,0:T(8,128)(2,1)}), bf16[8,8,128,128]{3,2,1,0:T(8,128)(2,1)}, u32[]{:S(2)}, u32[]{:S(2)}) async-start(bf16[8,8,128,128]{3,2,1,0:T(8,128)(2,1)} %fusion.16), calls=%async_computation.1 | async-start | bytes 4194304 | tf_op jit(solution)/shard_map/all_to_all | solution.py:45
  161.0 65.5 %all_gather.3 = f32[64,128]{1,0:T(8,128)S(1)} all-gather(f32[8,128]{1,0:T(8,128)S(1)} %copy-done.1), channel_id=1, replica_groups=mesh['seq'=32,'head'=8] {'head'}, dimensions={0}, use_global_device_ids=true | all-gather | bytes 36864 | tf_op jit(solution)/shard_map/all_gather | solution.py:38
  226.5 5.1 %fusion.1 = f32[64,128,128]{2,1,0:T(8,128)} fusion(bf16[64,128,128]{2,1,0:T(8,128)(2,1)} %bitcast.21, bf16[128,8192]{1,0:T(8,128)(2,1)S(1)} %copy-done), kind=kOutput, calls=%fused_computation.5 | convolution fusion | flops 268435456 | bytes 8388608 | tf_op jit(solution)/shard_map/bhd,hde->bhe/dot_general | solution.py:47
  231.7 7.6 %multiply_reduce_fusion = (f32[128,64]{0,1:T(8,128)S(1)}, f32[128,64,128]{0,2,1:T(8,128)}) fusion(bf16[128,64,128]{0,2,1:T(8,128)(2,1)} %bitcast.111, bf16[128,64,128]{0,2,1:T(8,128)(2,1)} %bitcast.109, pred[128,128]{1,0:T(8,128)(4,1)S(1)} %iota_compare_fusion, f32[64,128,128]{2,1,0:T(8,128)} %fusion.1, bf16[128,8192]{1,0:T(8,128)(2,1)S(1)} %copy-done), kind=kOutput, calls=%fused_computation.2 | convolution fusion | flops 542105600 | bytes 14729216 | tf_op jit(solution)/shard_map/hbc,chd->bhd/dot_general | solution.py:51
  239.2 3.9 %multiply_convert_fusion = bf16[128,64,128]{0,2,1:T(8,128)(2,1)} fusion(f32[128,64,128]{0,2,1:T(8,128)} %get-tuple-element.10, f32[64,128]{1,0:T(8,128)S(1)} %all_gather.3, f32[128,64]{0,1:T(8,128)S(1)} %add_rsqrt_fusion), kind=kLoop, calls=%fused_computation.1 | loop fusion | flops 3145728 | bytes 6356992 | tf_op jit(solution)/shard_map/convert_element_type | solution.py:54
  243.1 4.1 %copy.10 = bf16[128,8192]{1,0:T(8,128)(2,1)} copy(bf16[128,8192]{0,1:T(8,128)(2,1)} %bitcast.112) | data formatting | bytes 4194304 | tf_op jit(solution)/shard_map/reshape | solution.py:55
  (20 shorter events, 5.8 us)
Async XLA Ops:
  0.0 226.5 %copy-start = (bf16[128,8192]{1,0:T(8,128)(2,1)S(1)}, bf16[128,8192]{1,0:T(8,128)(2,1)}, u32[]{:S(2)}) copy-start(bf16[128,8192]{1,0:T(8,128)(2,1)} %param.4) | copy-start | bytes 6291460
  70.5 12.6 %collective-permute-start = (f32[8,128,128]{2,1,0:T(8,128)S(1)}, f32[8,128,128]{2,1,0:T(8,128)S(1)}, u32[]{:S(2)}, u32[]{:S(2)}) collective-permute-start(f32[8,128,128]{2,1,0:T(8,128)S(1)} %convert_reduce_fusion), channel_id=1, source_target_pairs={{0,8},{8,16},{16,24},{24,32},{32,40},{40,48},{48,56},{56,64},{64,7... | collective-permute-start | bytes 1572872 | tf_op jit(solution)/shard_map/ppermute | solution.py:12
  83.2 14.8 %collective-permute-start.1 = (f32[8,128,128]{2,1,0:T(8,128)S(1)}, f32[8,128,128]{2,1,0:T(8,128)S(1)}, u32[]{:S(2)}, u32[]{:S(2)}) collective-permute-start(f32[8,128,128]{2,1,0:T(8,128)S(1)} %add.50), channel_id=1, source_target_pairs={{0,16},{8,24},{16,32},{24,40},{32,48},{40,56},{48,64},{56,72},{64,... | collective-permute-start | bytes 1572872 | tf_op jit(solution)/shard_map/ppermute | solution.py:12
  98.1 14.3 %collective-permute-start.2 = (f32[8,128,128]{2,1,0:T(8,128)S(1)}, f32[8,128,128]{2,1,0:T(8,128)S(1)}, u32[]{:S(2)}, u32[]{:S(2)}) collective-permute-start(f32[8,128,128]{2,1,0:T(8,128)S(1)} %add.51), channel_id=1, source_target_pairs={{0,32},{8,40},{16,48},{24,56},{32,64},{40,72},{48,80},{56,88},{64,... | collective-permute-start | bytes 1572872 | tf_op jit(solution)/shard_map/ppermute | solution.py:12
  112.5 11.2 %collective-permute-start.3 = (f32[8,128,128]{2,1,0:T(8,128)S(1)}, f32[8,128,128]{2,1,0:T(8,128)S(1)}, u32[]{:S(2)}, u32[]{:S(2)}) collective-permute-start(f32[8,128,128]{2,1,0:T(8,128)S(1)} %add.52), channel_id=1, source_target_pairs={{0,64},{8,72},{16,80},{24,88},{32,96},{40,104},{48,112},{56,120},{... | collective-permute-start | bytes 1572872 | tf_op jit(solution)/shard_map/ppermute | solution.py:12
  123.7 12.6 %collective-permute-start.4 = (f32[8,128,128]{2,1,0:T(8,128)S(1)}, f32[8,128,128]{2,1,0:T(8,128)S(1)}, u32[]{:S(2)}, u32[]{:S(2)}) collective-permute-start(f32[8,128,128]{2,1,0:T(8,128)S(1)} %add.53), channel_id=1, source_target_pairs={{0,128},{8,136},{16,144},{24,152},{32,160},{40,168},{48,176},{56,1... | collective-permute-start | bytes 1572872 | tf_op jit(solution)/shard_map/ppermute | solution.py:12
  136.3 12.6 %collective-permute-start.5 = (f32[8,128,128]{2,1,0:T(8,128)S(1)}, f32[8,128,128]{2,1,0:T(8,128)S(1)}, u32[]{:S(2)}, u32[]{:S(2)}) collective-permute-start(f32[8,128,128]{2,1,0:T(8,128)S(1)} %add.54), channel_id=1, source_target_pairs={{0,8},{8,16},{16,24},{24,32},{32,40},{40,48},{48,56},{56,64},{64,7... | collective-permute-start | bytes 1572872 | tf_op jit(solution)/shard_map/ppermute | solution.py:12
  155.2 5.8 %copy-start.1 = (f32[8,128]{1,0:T(8,128)S(1)}, f32[8,128]{1,0:T(8,128)}, u32[]{:S(2)}) copy-start(f32[8,128]{1,0:T(8,128)} %param.7) | copy-start | bytes 12292
  155.2 71.3 %all-to-all-start.1 = ((bf16[8,8,128,128]{3,2,1,0:T(8,128)(2,1)}), bf16[8,8,128,128]{3,2,1,0:T(8,128)(2,1)}, u32[]{:S(2)}, u32[]{:S(2)}) async-start(bf16[8,8,128,128]{3,2,1,0:T(8,128)(2,1)} %fusion.16), calls=%async_computation.1 | async-start | bytes 4194304 | tf_op jit(solution)/shard_map/all_to_all | solution.py:45
where the time goes:
time: 248 us; the launch traced here: 247 us
  blocking collectives  124 us (50%)
  waiting for transfers between devices  66.7 us (27%)
  starting transfers between devices  16.7 us (7%)
  matrix products  16.5 us (7%)
  local copies, waits for them, and re-layouts  12.3 us (5%)
  other arithmetic  11.3 us (5%)
    ppermute x6, waiting for transfers between devices, shifted(): lax.ppermute(block, axis, [(i, i + distance) for i in range(count - dista...  66.7 us
    all_gather x1, blocking collectives, per_device(): gain = lax.all_gather(out_gain, 'head', axis=0, tiled=True)  65.5 us
    all_to_all x1, blocking collectives, per_device(): lax.all_to_all(states.astype(jnp.bfloat16).reshape(8, HEADS // 8, HD, HD)...  58.1 us
    ppermute x6, starting transfers between devices, shifted(): lax.ppermute(block, axis, [(i, i + distance) for i in range(count - dista...  10.9 us
    dot_general x1, matrix products, per_device(): jnp.einsum('hbc,chd->bhd', scores, value_heads, preferred_element_type=jn...  7.56 us
    all_to_all x1, starting transfers between devices, per_device(): lax.all_to_all(jnp.stack(parts), 'head', split_axis=0, concat_axis=0, til...  5.8 us
    unnamed x7, other arithmetic  5.4 us
    dot_general x1, matrix products, per_device(): jnp.einsum('bhd,hde->bhe', query_heads, carried, preferred_element_type=j...  5.14 us
  transfers between devices with their start and end apart: 7, of which 6 were waited for; matrix products, arithmetic and copies ran while one was open for 0% of the time, Pallas kernels for 0%

commit v1 on v0

--- a/solution.py
+++ b/solution.py
@@ -5,6 +5,10 @@
 
 HEADS = 64
 HD = 128
+sample_press = lambda t0, array_dim: jnp.concatenate(
+    lax.all_to_all(jnp.stack([t0 for _ in range(lax.axis_size("head"))], axis=0), "head", 0, 0),
+    axis=array_dim,
+)
 
 
 def shifted(block, axis, distance):
@@ -35,7 +39,7 @@
         concat_axis=0,
         tiled=True,
     ).astype(jnp.float32)
-    gain = lax.all_gather(out_gain, "head", axis=0, tiled=True)
+    gain = sample_press(out_gain, 0)
     prefix = seq_exclusive(jnp.sum(gathered, axis=0))
     running = prefix
     parts = []

time: 248 us -> 236 us (0.952)
  blocking collectives: 124 us -> 58.1 us
  waiting for transfers between devices: 66.7 us -> 115 us
  starting transfers between devices: 16.7 us -> 21.4 us
    all_gather x1 -> x0, blocking collectives: 65.5 us -> none  [per_device(): gain = lax.all_gather(out_gain, 'head', axis=0, tiled=True)]
    all_to_all x1, waiting for transfers between devices: 0.01 us -> 48.6 us  [per_device(): lax.all_to_all(jnp.stack(parts), 'head', split_axis=0, concat_axis=0, til...]
    all_to_all x0 -> x1, starting transfers between devices: none -> 4.73 us  [lax.all_to_all(jnp.stack([t0 for _ in range(lax.axis_size('head'))], axis...]
  transfers between devices with their start and end apart: 7 -> 8, of which waited for: 6 -> 7; matrix products, arithmetic and copies ran while one was open for 0% -> 6% of each run, Pallas kernels for 0% -> 0%
where the time goes in v1:
time: 236 us
  waiting for transfers between devices  115 us (49%)
  blocking collectives  58.1 us (25%)
  starting transfers between devices  21.4 us (9%)
  matrix products  16.5 us (7%)
  local copies, waits for them, and re-layouts  13 us (6%)
  other arithmetic  11.3 us (5%)
    ppermute x6, waiting for transfers between devices, shifted(): lax.ppermute(block, axis, [(i, i + distance) for i in range(count - dista...  66.7 us
    all_to_all x1, blocking collectives, per_device(): lax.all_to_all(states.astype(jnp.bfloat16).reshape(8, HEADS // 8, HD, HD)...  58.1 us
    all_to_all x1, waiting for transfers between devices, per_device(): lax.all_to_all(jnp.stack(parts), 'head', split_axis=0, concat_axis=0, til...  48.6 us
    ppermute x6, starting transfers between devices, shifted(): lax.ppermute(block, axis, [(i, i + distance) for i in range(count - dista...  10.9 us
    dot_general x1, matrix products, per_device(): jnp.einsum('hbc,chd->bhd', scores, value_heads, preferred_element_type=jn...  7.56 us
    all_to_all x1, starting transfers between devices, per_device(): lax.all_to_all(jnp.stack(parts), 'head', split_axis=0, concat_axis=0, til...  5.81 us
    unnamed x7, other arithmetic  5.43 us
    dot_general x1, matrix products, per_device(): jnp.einsum('bhd,hde->bhe', query_heads, carried, preferred_element_type=j...  5.15 us
  transfers between devices with their start and end apart: 8, of which 7 were waited for; matrix products, arithmetic and copies ran while one was open for 6% of the time, Pallas kernels for 0%

profile of v1, /device:TPU:56, one launch (start us, length us, event | category | flops | bytes accessed | tf_op | source)
XLA Modules:
  0.0 235.6 jit_solution(2183062496052886105)
XLA Ops:
  0.0 4.2 %copy.11 = bf16[128,8192]{0,1:T(8,128)(2,1)} copy(bf16[128,8192]{1,0:T(8,128)(2,1)} %param.5) | data formatting | bytes 4194304 | tf_op jit(solution)/shard_map/reshape | solution.py:32
  4.2 4.1 %copy.12 = bf16[128,8192]{0,1:T(8,128)(2,1)} copy(bf16[128,8192]{1,0:T(8,128)(2,1)} %param.6) | data formatting | bytes 4194304 | tf_op jit(solution)/shard_map/reshape | solution.py:33
  8.3 3.8 %convolution_convert_fusion = bf16[64,128,128]{2,1,0:T(8,128)(2,1)S(1)} fusion(bf16[128,64,128]{0,2,1:T(8,128)(2,1)} %bitcast.109, bf16[128,64,128]{0,2,1:T(8,128)(2,1)} %bitcast.111), kind=kOutput, calls=%fused_computation.7 | convolution fusion | flops 269484032 | bytes 6291456 | tf_op jit(solution)/shard_map/bhd,bhe->hde/dot_general | solution.py:34
  12.1 58.1 %all_to_all.15 = bf16[8,8,128,128]{3,2,1,0:T(8,128)(2,1)S(1)} all-to-all(bf16[8,8,128,128]{3,2,1,0:T(8,128)(2,1)S(1)} %bitcast.114), channel_id=1, replica_groups=mesh['seq'=32,'head'=8] {'head'}, dimensions={0} | all-to-all | bytes 4194304 | tf_op jit(solution)/shard_map/all_to_all | solution.py:35
  70.5 1.9 collective-permute-start
  72.5 10.7 %collective-permute-done = f32[8,128,128]{2,1,0:T(8,128)S(1)} collective-permute-done((f32[8,128,128]{2,1,0:T(8,128)S(1)}, f32[8,128,128]{2,1,0:T(8,128)S(1)}, u32[]{:S(2)}, u32[]{:S(2)}) %collective-permute-start) | collective-permute-done | bytes 524320 | tf_op jit(solution)/shard_map/ppermute | solution.py:16
  83.2 1.9 collective-permute-start.1
  85.1 12.9 %collective-permute-done.1 = f32[8,128,128]{2,1,0:T(8,128)S(1)} collective-permute-done((f32[8,128,128]{2,1,0:T(8,128)S(1)}, f32[8,128,128]{2,1,0:T(8,128)S(1)}, u32[]{:S(2)}, u32[]{:S(2)}) %collective-permute-start.1) | collective-permute-done | bytes 524320 | tf_op jit(solution)/shard_map/ppermute | solution.py:16
  98.1 2.5 %collective-permute-start.2 = (f32[8,128,128]{2,1,0:T(8,128)S(1)}, f32[8,128,128]{2,1,0:T(8,128)S(1)}, u32[]{:S(2)}, u32[]{:S(2)}) collective-permute-start(f32[8,128,128]{2,1,0:T(8,128)S(1)} %add.51), channel_id=1, source_target_pairs={{0,32},{8,40},{16,48},{24,56},{32,64},{40,72},{48,80},{56,88},{64,... | collective-permute-start | bytes 1572872 | tf_op jit(solution)/shard_map/ppermute | solution.py:16
  100.7 11.8 %collective-permute-done.2 = f32[8,128,128]{2,1,0:T(8,128)S(1)} collective-permute-done((f32[8,128,128]{2,1,0:T(8,128)S(1)}, f32[8,128,128]{2,1,0:T(8,128)S(1)}, u32[]{:S(2)}, u32[]{:S(2)}) %collective-permute-start.2) | collective-permute-done | bytes 524320 | tf_op jit(solution)/shard_map/ppermute | solution.py:16
  112.5 1.3 collective-permute-start.3
  113.8 9.9 %collective-permute-done.3 = f32[8,128,128]{2,1,0:T(8,128)S(1)} collective-permute-done((f32[8,128,128]{2,1,0:T(8,128)S(1)}, f32[8,128,128]{2,1,0:T(8,128)S(1)}, u32[]{:S(2)}, u32[]{:S(2)}) %collective-permute-start.3) | collective-permute-done | bytes 524320 | tf_op jit(solution)/shard_map/ppermute | solution.py:16
  123.7 1.3 collective-permute-start.4
  125.0 11.3 %collective-permute-done.4 = f32[8,128,128]{2,1,0:T(8,128)S(1)} collective-permute-done((f32[8,128,128]{2,1,0:T(8,128)S(1)}, f32[8,128,128]{2,1,0:T(8,128)S(1)}, u32[]{:S(2)}, u32[]{:S(2)}) %collective-permute-start.4) | collective-permute-done | bytes 524320 | tf_op jit(solution)/shard_map/ppermute | solution.py:16
  136.3 1.9 collective-permute-start.5
  138.8 10.2 %collective-permute-done.5 = f32[8,128,128]{2,1,0:T(8,128)S(1)} collective-permute-done((f32[8,128,128]{2,1,0:T(8,128)S(1)}, f32[8,128,128]{2,1,0:T(8,128)S(1)}, u32[]{:S(2)}, u32[]{:S(2)}) %collective-permute-start.5) | collective-permute-done | bytes 524320 | tf_op jit(solution)/shard_map/ppermute | solution.py:16
  154.4 0.8 fusion.16
  155.2 5.8 %all-to-all-start.1 = ((bf16[8,8,128,128]{3,2,1,0:T(8,128)(2,1)}), bf16[8,8,128,128]{3,2,1,0:T(8,128)(2,1)}, u32[]{:S(2)}, u32[]{:S(2)}) async-start(bf16[8,8,128,128]{3,2,1,0:T(8,128)(2,1)} %fusion.16), calls=%async_computation.1 | async-start | bytes 4194304 | tf_op jit(solution)/shard_map/all_to_all | solution.py:49
  161.1 48.6 %all-to-all-done.1 = bf16[8,8,128,128]{3,2,1,0:T(8,128)(2,1)} async-done(((bf16[8,8,128,128]{3,2,1,0:T(8,128)(2,1)}), bf16[8,8,128,128]{3,2,1,0:T(8,128)(2,1)}, u32[]{:S(2)}, u32[]{:S(2)}) %all-to-all-start.1) | async-done | bytes 2097184 | tf_op jit(solution)/shard_map/all_to_all | solution.py:49
  210.2 4.7 %all-to-all-start.2 = ((f32[8,8,128]{2,1,0:T(8,128)}), f32[8,8,128]{2,1,0:T(8,128)S(1)}, u32[]{:S(2)}, u32[]{:S(2)}) async-start(f32[8,8,128]{2,1,0:T(8,128)} %stack.47), calls=%async_computation.2 | async-start | bytes 65536 | tf_op jit(solution)/shard_map/all_to_all | solution.py:9
  215.0 5.2 %fusion.1 = f32[64,128,128]{2,1,0:T(8,128)} fusion(bf16[64,128,128]{2,1,0:T(8,128)(2,1)} %bitcast.22, bf16[128,8192]{1,0:T(8,128)(2,1)S(1)} %copy-done), kind=kOutput, calls=%fused_computation.5 | convolution fusion | flops 268435456 | bytes 8388608 | tf_op jit(solution)/shard_map/bhd,hde->bhe/dot_general | solution.py:51
  220.1 7.6 %multiply_reduce_fusion = (f32[128,64]{0,1:T(8,128)S(1)}, f32[128,64,128]{0,2,1:T(8,128)}) fusion(bf16[128,64,128]{0,2,1:T(8,128)(2,1)} %bitcast.112, bf16[128,64,128]{0,2,1:T(8,128)(2,1)} %bitcast.110, pred[128,128]{1,0:T(8,128)(4,1)S(1)} %iota_compare_fusion, f32[64,128,128]{2,1,0:T(8,128)} %fusion.1, bf16[128,8192]{1,0:T(8,128)(2,1)S(1)} %copy-done), kind=kOutput, calls=%fused_computation.2 | convolution fusion | flops 542105600 | bytes 14729216 | tf_op jit(solution)/shard_map/hbc,chd->bhd/dot_general | solution.py:55
  227.7 3.8 %multiply_convert_fusion = bf16[128,64,128]{0,2,1:T(8,128)(2,1)} fusion(f32[128,64,128]{0,2,1:T(8,128)} %get-tuple-element.10, f32[64,128]{1,0:T(8,128)S(1)} %bitcast.115, f32[128,64]{0,1:T(8,128)S(1)} %add_rsqrt_fusion), kind=kLoop, calls=%fused_computation.1 | loop fusion | flops 3145728 | bytes 6356992 | tf_op jit(solution)/shard_map/convert_element_type | solution.py:58
  231.6 4.1 %copy.10 = bf16[128,8192]{1,0:T(8,128)(2,1)} copy(bf16[128,8192]{0,1:T(8,128)(2,1)} %bitcast.113) | data formatting | bytes 4194304 | tf_op jit(solution)/shard_map/reshape | solution.py:59
  (22 shorter events, 7.2 us)
Async XLA Ops:
  0.0 215.0 %copy-start = (bf16[128,8192]{1,0:T(8,128)(2,1)S(1)}, bf16[128,8192]{1,0:T(8,128)(2,1)}, u32[]{:S(2)}) copy-start(bf16[128,8192]{1,0:T(8,128)(2,1)} %param.4) | copy-start | bytes 6291460
  70.5 12.6 %collective-permute-start = (f32[8,128,128]{2,1,0:T(8,128)S(1)}, f32[8,128,128]{2,1,0:T(8,128)S(1)}, u32[]{:S(2)}, u32[]{:S(2)}) collective-permute-start(f32[8,128,128]{2,1,0:T(8,128)S(1)} %convert_reduce_fusion), channel_id=1, source_target_pairs={{0,8},{8,16},{16,24},{24,32},{32,40},{40,48},{48,56},{56,64},{64,7... | collective-permute-start | bytes 1572872 | tf_op jit(solution)/shard_map/ppermute | solution.py:16
  83.2 14.8 %collective-permute-start.1 = (f32[8,128,128]{2,1,0:T(8,128)S(1)}, f32[8,128,128]{2,1,0:T(8,128)S(1)}, u32[]{:S(2)}, u32[]{:S(2)}) collective-permute-start(f32[8,128,128]{2,1,0:T(8,128)S(1)} %add.50), channel_id=1, source_target_pairs={{0,16},{8,24},{16,32},{24,40},{32,48},{40,56},{48,64},{56,72},{64,... | collective-permute-start | bytes 1572872 | tf_op jit(solution)/shard_map/ppermute | solution.py:16
  98.1 14.3 %collective-permute-start.2 = (f32[8,128,128]{2,1,0:T(8,128)S(1)}, f32[8,128,128]{2,1,0:T(8,128)S(1)}, u32[]{:S(2)}, u32[]{:S(2)}) collective-permute-start(f32[8,128,128]{2,1,0:T(8,128)S(1)} %add.51), channel_id=1, source_target_pairs={{0,32},{8,40},{16,48},{24,56},{32,64},{40,72},{48,80},{56,88},{64,... | collective-permute-start | bytes 1572872 | tf_op jit(solution)/shard_map/ppermute | solution.py:16
  112.5 11.2 %collective-permute-start.3 = (f32[8,128,128]{2,1,0:T(8,128)S(1)}, f32[8,128,128]{2,1,0:T(8,128)S(1)}, u32[]{:S(2)}, u32[]{:S(2)}) collective-permute-start(f32[8,128,128]{2,1,0:T(8,128)S(1)} %add.52), channel_id=1, source_target_pairs={{0,64},{8,72},{16,80},{24,88},{32,96},{40,104},{48,112},{56,120},{... | collective-permute-start | bytes 1572872 | tf_op jit(solution)/shard_map/ppermute | solution.py:16
  123.7 12.6 %collective-permute-start.4 = (f32[8,128,128]{2,1,0:T(8,128)S(1)}, f32[8,128,128]{2,1,0:T(8,128)S(1)}, u32[]{:S(2)}, u32[]{:S(2)}) collective-permute-start(f32[8,128,128]{2,1,0:T(8,128)S(1)} %add.53), channel_id=1, source_target_pairs={{0,128},{8,136},{16,144},{24,152},{32,160},{40,168},{48,176},{56,1... | collective-permute-start | bytes 1572872 | tf_op jit(solution)/shard_map/ppermute | solution.py:16
  136.3 12.6 %collective-permute-start.5 = (f32[8,128,128]{2,1,0:T(8,128)S(1)}, f32[8,128,128]{2,1,0:T(8,128)S(1)}, u32[]{:S(2)}, u32[]{:S(2)}) collective-permute-start(f32[8,128,128]{2,1,0:T(8,128)S(1)} %add.54), channel_id=1, source_target_pairs={{0,8},{8,16},{16,24},{24,32},{32,40},{40,48},{48,56},{56,64},{64,7... | collective-permute-start | bytes 1572872 | tf_op jit(solution)/shard_map/ppermute | solution.py:16
  155.2 54.4 %copy-start.1 = (f32[8,128]{1,0:T(8,128)S(1)}, f32[8,128]{1,0:T(8,128)}, u32[]{:S(2)}) copy-start(f32[8,128]{1,0:T(8,128)} %param.7) | copy-start | bytes 12292
  155.2 54.4 %all-to-all-start.1 = ((bf16[8,8,128,128]{3,2,1,0:T(8,128)(2,1)}), bf16[8,8,128,128]{3,2,1,0:T(8,128)(2,1)}, u32[]{:S(2)}, u32[]{:S(2)}) async-start(bf16[8,8,128,128]{3,2,1,0:T(8,128)(2,1)} %fusion.16), calls=%async_computation.1 | async-start | bytes 4194304 | tf_op jit(solution)/shard_map/all_to_all | solution.py:49
  210.2 17.5 %all-to-all-start.2 = ((f32[8,8,128]{2,1,0:T(8,128)}), f32[8,8,128]{2,1,0:T(8,128)S(1)}, u32[]{:S(2)}, u32[]{:S(2)}) async-start(f32[8,8,128]{2,1,0:T(8,128)} %stack.47), calls=%async_computation.2 | async-start | bytes 65536 | tf_op jit(solution)/shard_map/all_to_all | solution.py:9
